TPU v7x, 32 devices: a whole 2x2x4 slice. The times are simulated.
32 devices in a mesh: pp: 4 (over y, x), cp: 4 (over z), tp: 2 (over core).
Axes of the slice: x: 2, y: 2, z: 4, core: 2. Of those that a mesh axis runs over, the one named last changes fastest.
Arguments:
- queries: bfloat16 [2048, 16384], P(('pp', 'cp'), 'tp'), may hold values from -12 to 12
- keys: bfloat16 [2048, 1024], P(('pp', 'cp'), 'tp'), may hold values from -12 to 12
- values: bfloat16 [2048, 1024], P(('pp', 'cp'), 'tp'), may hold values from -6 to 6
- pair_order: int32 [4, 4], replicated, may hold values from 0 to 3, each once within a row
- lengths: int32 [4, 2], replicated, may hold values from 128 to 256
- routes: int32 [4, 512, 1], P(None, 'cp'), may hold values from 0 to 7; in each aligned block of 128 rows (0 to 127, 128 to 255, ..., all dimensions but the last counted through in order) at most 32 rows name the same one
Outputs:
- rebalanced: bfloat16 [4096, 16384], P(('pp', 'cp', 'tp'))
Inputs may be any that keep to these rules, and one draw needn't show every extreme that they name: `routes`: at most 32 rows of one device's block name the same destination, and in some block one destination is named by exactly 32 rows.
All inputs are finite; a program needn't handle non-finite values.
Results may differ from a plain program's by a relative error of at most 0.003.
Values may be sent and summed in bfloat16 or wider, within the bound.
No kernel may reach another device: no remote copies, remote signals or barrier semaphores. Data moves between devices by JAX's collectives and lax.ppermute only.
A program may use at most 64 MiB of HBM per device.

v0:
```python
import jax
import jax.numpy as jnp
from jax import lax
from jax.sharding import PartitionSpec as P

HD = 128
masked_score = -1e30


def shifted(block, axis, distance):
    devices = range(lax.axis_size(axis))
    route = [((i - distance) % len(devices), i) for i in devices]
    return lax.ppermute(block, axis, route)


def pair_positions(pair_ids, block_len, cycle_size):
    offsets = jnp.arange(block_len, dtype=jnp.int32)
    first_half = pair_ids[:, None] * block_len + offsets[None, :]
    second_half = (2 * cycle_size - 1 - pair_ids)[:, None] * block_len + offsets[None, :]
    return jnp.concatenate([first_half, second_half], axis=1)


def dispatch_rows(attended, targets, dest_count, capacity):
    row_count = attended.shape[0]
    matches = targets[:, None] == jnp.arange(dest_count, dtype=jnp.int32)[None, :]
    row_ids = jnp.arange(row_count, dtype=jnp.int32)
    earlier = (row_ids[None, :] < row_ids[:, None]).astype(jnp.bfloat16)
    before = jnp.dot(earlier, matches.astype(jnp.bfloat16), preferred_element_type=jnp.float32)
    slot_index = jnp.sum(jnp.where(matches, before, 0.0), axis=1).astype(jnp.int32)
    slot_ids = jnp.arange(capacity, dtype=jnp.int32)
    picked_rows = jnp.logical_and(
        jnp.transpose(matches)[:, None, :], slot_index[None, None, :] == slot_ids[None, :, None]
    )
    selector = picked_rows.astype(jnp.bfloat16).reshape(dest_count * capacity, row_count)
    return jnp.dot(selector, attended, preferred_element_type=jnp.float32).astype(jnp.bfloat16)


def spread_rows(buffer, cycle_size, split_size, capacity, width):
    flat_buffer = buffer.reshape(cycle_size * split_size, capacity, width)
    moved = lax.all_to_all(flat_buffer, ("cp", "tp"), split_axis=0, concat_axis=0, tiled=True)
    moved = jnp.transpose(moved.reshape(cycle_size, split_size, capacity, width), (0, 2, 1, 3))
    return moved.reshape(cycle_size * capacity, split_size * width)


def arrange_rows(attended, routes, source, cycle_size, split_size):
    row_count, width = attended.shape
    dest_count = cycle_size * split_size
    capacity = 2 * row_count // dest_count
    targets = lax.dynamic_index_in_dim(routes, source, 0, keepdims=False)[:, 0]
    buffer = dispatch_rows(attended, targets, dest_count, capacity)
    buffer = buffer.reshape(cycle_size, split_size, capacity, width)
    return spread_rows(buffer, cycle_size, split_size, capacity, width)


def body(queries, keys, values, pair_order, lengths, routes):
    cycle_size = lax.axis_size("cp")
    split_size = lax.axis_size("tp")
    section = lax.axis_index("pp")
    place = lax.axis_index("cp")
    row_count = queries.shape[0]
    block_len = row_count // 4
    width = queries.shape[1]
    group_count = keys.shape[1] // HD
    group_size = width // keys.shape[1]
    score_scale = HD ** (-0.5)
    order_row = lax.dynamic_index_in_dim(pair_order, section, 0, keepdims=False)
    own_pair = lax.dynamic_index_in_dim(order_row, place, 0, keepdims=True)
    query_pos = pair_positions(own_pair, block_len, cycle_size).reshape(2 * block_len)
    limits = lax.dynamic_index_in_dim(lengths, section, 0, keepdims=False)
    query_rows = queries.reshape(2, 2 * block_len, group_count, group_size, HD)
    stat_shape = (2, 2 * block_len, group_count, group_size)
    start_state = (
        jnp.full(stat_shape, masked_score, jnp.float32),
        jnp.zeros(stat_shape, jnp.float32),
        jnp.zeros(stat_shape + (HD,), jnp.float32),
    )
    state = start_state
    key_piece = lax.all_gather(keys, "cp", axis=0, tiled=True)
    value_piece = lax.all_gather(values, "cp", axis=0, tiled=True)
    shard_count = key_piece.shape[0] // row_count
    first_shard = jnp.int32(0) // row_count
    for base in range(0, shard_count, 4):
        block = min(4, shard_count - base)
        key_block = key_piece[base * row_count : (base + block) * row_count].reshape(
            block, 2, 2 * block_len, group_count, HD
        )
        value_block = value_piece[base * row_count : (base + block) * row_count].reshape(
            block, 2, 2 * block_len, group_count, HD
        )
        shard_ids = first_shard + base + jnp.arange(block, dtype=jnp.int32)
        key_pos = pair_positions(order_row[shard_ids], block_len, cycle_size).reshape(
            block * 2 * block_len
        )
        allowed = jnp.logical_and(
            key_pos[None, None, :] <= query_pos[None, :, None],
            key_pos[None, None, :] < limits[:, None, None],
        )
        allowed = allowed[:, :, None, None, :]
        scores = jnp.einsum(
            "sqgrd,nskgd->sqgrnk", query_rows, key_block, preferred_element_type=jnp.float32
        )
        scores = scores.reshape(stat_shape + (block * 2 * block_len,)) * score_scale
        running_max, running_total, running_sum = state
        block_max = jnp.max(jnp.where(allowed, scores, masked_score), axis=4)
        new_max = jnp.maximum(running_max, block_max)
        weights = jnp.where(allowed, jnp.exp(scores - new_max[..., None]), 0.0)
        carry_factor = jnp.exp(running_max - new_max)
        running_total = running_total * carry_factor + jnp.sum(weights, axis=4)
        shaped = weights.astype(jnp.bfloat16).reshape(stat_shape + (block, 2 * block_len))
        running_sum = running_sum * carry_factor[..., None] + jnp.einsum(
            "sqgrnk,nskgd->sqgrd", shaped, value_block, preferred_element_type=jnp.float32
        )
        state = (new_max, running_total, running_sum)
    attended = (state[2] / state[1][..., None]).astype(jnp.bfloat16).reshape(row_count, width)
    arranged = arrange_rows(attended, routes, section, cycle_size, split_size)
    return shifted(arranged, "pp", 1)


def solution(mesh):
    placed = (
        P(("pp", "cp"), "tp"),
        P(("pp", "cp"), "tp"),
        P(("pp", "cp"), "tp"),
        P(),
        P(),
        P(None, "cp", None),
    )
    return jax.shard_map(
        body, mesh=mesh, in_specs=placed, out_specs=P(("pp", "cp", "tp"), None), check_vma=False
    )
```

profile of v0, /device:TPU:0, one launch (start us, length us, event | category | flops | bytes accessed | tf_op | source)
XLA Modules:
  0.0 287.3 jit_solution(959507155664328261)
XLA Ops:
  0.0 0.7 copy-done
  0.7 0.1 fusion.9
  0.9 0.7 fusion.14
  1.6 1.3 dynamic_slice.18
  4.1 0.6 gather_fusion
  4.8 0.9 dynamic-slice_reduce_fusion
  5.7 0.1 add_bitcast_fusion
  5.7 0.1 iota_add_fusion
  5.8 0.1 pad_add_fusion
  5.9 0.1 broadcast_compare_fusion
  6.0 0.1 broadcast_compare_fusion.1
  6.1 2.2 copy.30
  8.3 17.4 %all_gather.6 = bf16[512,512]{1,0:T(8,128)(2,1)S(1)} all-gather(bf16[128,512]{1,0:T(8,128)(2,1)S(1)} %copy-done.2), channel_id=1, replica_groups=mesh['pp'=4,'cp'=4,'tp'=2] {'cp'}, dimensions={0}, use_global_device_ids=true | all-gather | bytes 655360 | tf_op jit(solution)/shard_map/all_gather | solution.py:78
  25.6 0.1 reshape.234
  25.8 0.1 broadcast_and_fusion
  25.9 5.5 %fusion = (f32[2,64,4,16]{1,3,2,0:T(8,128)S(1)}, f32[2,4,4,64,64,16]{4,3,5,2,1,0:T(8,128)S(1)}) fusion(pred[2,64,4,64]{1,3,2,0:T(8,128)(4,1)S(1)} %broadcast_and_fusion, bf16[2,64,4,16,128,1]{4,3,2,1,0,5:T(8,128)(2,1)S(1)} %bitcast.52, bf16[4,2,64,4,128,1]{4,3,2,1,0,5:T(4,128)(2,1)S(1)} %bitcast.54), kind=kOutput, calls=%fused_computation.3 | convolution fusion | flops 543154176 | bytes 11075584 | tf_op jit(solution)/shard_map/sqgrd,nskgd->sqgrnk/dot_general | solution.py:99
  31.4 6.2 %fusion.3 = (f32[2,64,4,16]{1,3,2,0:T(8,128)S(1)}, bf16[2,64,4,16,4,64]{1,5,3,4,2,0:T(8,128)(2,1)}) fusion(f32[2,4,4,64,64,16]{4,3,5,2,1,0:T(8,128)S(1)} %get-tuple-element.12, f32[2,64,4,16]{1,3,2,0:T(8,128)S(1)} %broadcast_maximum_fusion, pred[2,64,4,64]{1,3,2,0:T(8,128)(4,1)S(1)} %broadcast_and_fusion), kind=kLoop, calls=%fused_computation.6 | loop fusion | flops 10477568 | bytes 12681216 | tf_op jit(solution)/shard_map/reduce_sum | solution.py:108
  37.7 0.1 copy.14
  37.8 0.1 copy.17
  38.0 17.2 %copy.15 = bf16[2,64,4,16,4,64]{5,3,4,1,2,0:T(8,128)(2,1)} copy(bf16[2,64,4,16,4,64]{1,5,3,4,2,0:T(8,128)(2,1)} %get-tuple-element.6) | data formatting | bytes 8388608 | tf_op jit(solution)/shard_map/convert_element_type | solution.py:109
  55.2 16.2 %all_gather.7 = bf16[512,512]{1,0:T(8,128)(2,1)S(1)} all-gather(bf16[128,512]{1,0:T(8,128)(2,1)S(1)} %copy-done.3), channel_id=1, replica_groups=mesh['pp'=4,'cp'=4,'tp'=2] {'cp'}, dimensions={0}, use_global_device_ids=true | all-gather | bytes 655360 | tf_op jit(solution)/shard_map/all_gather | solution.py:79
  71.4 0.1 reshape.236
  71.6 5.7 %fusion.6 = bf16[2,64,4,16,128]{4,3,1,2,0:T(8,128)(2,1)S(1)} fusion(bf16[2,64,4,16,4,64]{5,3,4,1,2,0:T(8,128)(2,1)} %copy.15, f32[2,64,4,16]{3,1,2,0:T(8,128)S(1)} %copy.17, f32[2,64,4,16]{3,1,2,0:T(8,128)S(1)} %copy.14, bf16[4,2,64,4,128,1]{4,3,2,1,0,5:T(4,128)(2,1)S(1)} %bitcast.56), kind=kOutput, calls=%fused_computation.11 | convolution fusion | flops 540016640 | bytes 6881280 | tf_op jit(solution)/shard_map/sqgrnk,nskgd->sqgrd/dot_general | solution.py:110
  77.3 1.9 copy.18
  79.2 2.8 reshape.237
  82.1 1.2 convolution_convert_fusion
  83.3 97.9 %all_to_all.5 = bf16[8,32,8192]{2,1,0:T(8,128)(2,1)S(1)} all-to-all(bf16[8,32,8192]{2,1,0:T(8,128)(2,1)S(1)} %bitcast.49), channel_id=1, replica_groups=mesh['pp'=4,'cp'=4,'tp'=2] {'cp','tp'}, dimensions={0} | all-to-all | bytes 8388608 | tf_op jit(solution)/shard_map/all_to_all | solution.py:40
  181.2 6.4 %copy.19 = bf16[4,2,32,8192]{3,1,2,0:T(2,128)(2,1)} copy(bf16[4,2,32,8192]{3,2,1,0:T(8,128)(2,1)S(1)} %bitcast.50) | data formatting | bytes 8388608 | tf_op jit(solution)/shard_map/reshape | solution.py:41
  187.6 4.8 %copy.31 = bf16[16,8,2,8192]{3,1,2,0:T(8,128)(2,1)S(1)} copy(bf16[16,8,2,8192]{3,2,1,0:T(2,128)(2,1)} %bitcast.51) | data formatting | bytes 8388608
  192.4 1.6 collective-permute-start
  194.0 91.3 %collective-permute-done = bf16[128,16384]{1,0:T(8,128)(2,1)S(1)} collective-permute-done((bf16[128,16384]{1,0:T(8,128)(2,1)S(1)}, bf16[128,16384]{1,0:T(8,128)(2,1)S(1)}, u32[]{:S(2)}, u32[]{:S(2)}) %collective-permute-start) | collective-permute-done | bytes 4194336 | tf_op jit(solution)/shard_map/ppermute | solution.py:13
  285.3 2.0 copy.45
  (18 shorter events, 0.1 us)
Async XLA Ops:
  0.0 0.7 copy-start
  0.0 8.3 %copy-start.2 = (bf16[128,512]{1,0:T(8,128)(2,1)S(1)}, bf16[128,512]{1,0:T(8,128)(2,1)}, u32[]{:S(2)}) copy-start(bf16[128,512]{1,0:T(8,128)(2,1)} %param.7) | copy-start | bytes 393220
  38.0 17.2 %copy-start.3 = (bf16[128,512]{1,0:T(8,128)(2,1)S(1)}, bf16[128,512]{1,0:T(8,128)(2,1)}, u32[]{:S(2)}) copy-start(bf16[128,512]{1,0:T(8,128)(2,1)} %param.8) | copy-start | bytes 393220
  192.4 94.9 %copy-start.1 = (s32[4,128,1]{1,2,0:T(1,128)S(1)}, s32[4,128,1]{1,2,0:T(1,128)}, u32[]{:S(2)}) copy-start(s32[4,128,1]{1,2,0:T(1,128)} %param.11) | copy-start | bytes 6148
  192.4 92.9 %collective-permute-start = (bf16[128,16384]{1,0:T(8,128)(2,1)S(1)}, bf16[128,16384]{1,0:T(8,128)(2,1)S(1)}, u32[]{:S(2)}, u32[]{:S(2)}) collective-permute-start(bf16[128,16384]{1,0:T(8,128)(2,1)S(1)} %bitcast.53), channel_id=1, source_target_pairs={{24,0},{0,8},{8,16},{16,24},{25,1},{1,9},{9,17},{17,25},{26,2},{2,... | collective-permute-start | bytes 12582920 | tf_op jit(solution)/shard_map/ppermute | solution.py:13
where the time goes:
time: 288 us; the launch traced here: 287 us
  blocking collectives  131 us (45%)
  waiting for transfers between devices  91.3 us (32%)
  local copies, waits for them, and re-layouts  42 us (15%)
  matrix products  12.6 us (4%)
  other arithmetic  6.85 us (2%)
    all_to_all x1, blocking collectives, spread_rows(): lax.all_to_all(flat_buffer, ('cp', 'tp'), split_axis=0, concat_axis=0, ti...  97.9 us
    ppermute x1, waiting for transfers between devices, shifted(): return lax.ppermute(block, axis, route)  91.3 us
    all_gather x1, blocking collectives, body(): key_piece = lax.all_gather(keys, 'cp', axis=0, tiled=True)  17.4 us
    convert_element_type x1, local copies, waits for them, and re-layouts, body(): weights.astype(jnp.bfloat16).reshape(stat_shape + (block, 2 * block_len))  17.2 us
    all_gather x1, blocking collectives, body(): value_piece = lax.all_gather(values, 'cp', axis=0, tiled=True)  16.2 us
    unnamed x11, local copies, waits for them, and re-layouts  9.69 us
    reshape x1, local copies, waits for them, and re-layouts, spread_rows(): moved.reshape(cycle_size, split_size, capacity, width)  6.38 us
    reduce_sum x1, other arithmetic, body(): running_total = running_total * carry_factor + jnp.sum(weights, axis=4)  6.22 us
  transfers between devices with their start and end apart: 1, of which 1 were waited for; matrix products, arithmetic and copies ran while one was open for 0% of the time, Pallas kernels for 0%

commit v1 on v0

--- a/solution.py
+++ b/solution.py
@@ -75,8 +75,11 @@
         jnp.zeros(stat_shape + (HD,), jnp.float32),
     )
     state = start_state
-    key_piece = lax.all_gather(keys, "cp", axis=0, tiled=True)
-    value_piece = lax.all_gather(values, "cp", axis=0, tiled=True)
+    key_piece, value_piece = jnp.split(
+        lax.all_gather(jnp.concatenate([keys, values], axis=1), "cp", tiled=True, axis=0),
+        [keys.shape[1]],
+        axis=1,
+    )
     shard_count = key_piece.shape[0] // row_count
     first_shard = jnp.int32(0) // row_count
     for base in range(0, shard_count, 4):

time: 288 us -> 279 us (0.969)
  blocking collectives: 131 us -> 97 us
  waiting for transfers between devices: 91.3 us -> 115 us
  local copies, waits for them, and re-layouts: 42 us -> 27.7 us
  between operations: 1.49 us -> 14.8 us
    all_gather x2 -> x0, blocking collectives: 33.6 us -> none  [the longest x1 17.4 us: body(): key_piece = lax.all_gather(keys, 'cp', axis=0, tiled=True)]
    all_gather x0 -> x1, waiting for transfers between devices: none -> 23.6 us  [body(): lax.all_gather(jnp.concatenate([keys, values], axis=1), 'cp', tiled=True,...]
    convert_element_type x1 -> x0, local copies, waits for them, and re-layouts: 17.2 us -> none  [body(): weights.astype(jnp.bfloat16).reshape(stat_shape + (block, 2 * block_len))]
    unnamed x11 -> x5, local copies, waits for them, and re-layouts: 9.69 us -> 9 us
  transfers between devices with their start and end apart: 1 -> 2, of which waited for: 1 -> 2; matrix products, arithmetic and copies ran while one was open for 0% -> 2% of each run, Pallas kernels for 0% -> 0%
where the time goes in v1:
time: 279 us; the launch traced here: 278 us
  waiting for transfers between devices  115 us (41%)
  blocking collectives  97 us (35%)
  local copies, waits for them, and re-layouts  27.7 us (10%)
  between operations  14.8 us (5%)
  matrix products  13.7 us (5%)
  other arithmetic  8.54 us (3%)
    all_to_all x1, blocking collectives, spread_rows(): lax.all_to_all(flat_buffer, ('cp', 'tp'), split_axis=0, concat_axis=0, ti...  97 us
    ppermute x1, waiting for transfers between devices, shifted(): return lax.ppermute(block, axis, route)  91.4 us
    all_gather x1, waiting for transfers between devices, body(): lax.all_gather(jnp.concatenate([keys, values], axis=1), 'cp', tiled=True,...  23.6 us
    unnamed x5, local copies, waits for them, and re-layouts  9 us
    dot_general x1, matrix products, body(): jnp.einsum('sqgrnk,nskgd->sqgrd', shaped, value_block, preferred_element_...  6.76 us
    reshape x1, local copies, waits for them, and re-layouts, spread_rows(): moved.reshape(cycle_size, split_size, capacity, width)  6.38 us
    reduce_sum x1, other arithmetic, body(): running_total = running_total * carry_factor + jnp.sum(weights, axis=4)  6.21 us
  transfers between devices with their start and end apart: 2, of which 2 were waited for; matrix products, arithmetic and copies ran while one was open for 2% of the time, Pallas kernels for 0%

profile of v1, /device:TPU:0, one launch (start us, length us, event | category | flops | bytes accessed | tf_op | source)
XLA Modules:
  0.0 278.2 jit_solution(16795584549973656999)
XLA Ops:
  6.5 0.0 copy-start
  6.5 0.0 all-gather.2.cloned.1.call-start
  6.5 1.7 pad_maximum_fusion
  8.2 0.0 all-gather.2.cloned.1.call-update
  8.3 0.7 fusion.18
  9.0 1.3 dynamic_slice.18
  11.6 0.6 gather_fusion
  12.2 0.9 dynamic-slice_reduce_fusion
  13.1 2.2 copy.28
  15.3 0.2 fusion.13
  15.5 0.1 iota_add_fusion
  15.5 0.1 add_bitcast_fusion
  15.6 0.1 pad_add_fusion
  15.7 0.1 broadcast_compare_fusion.1
  15.8 0.1 broadcast_compare_fusion
  15.9 0.1 broadcast_and_fusion
  16.1 23.6 %all-gather.2.cloned.1.call-done = bf16[512,1024]{1,0:T(8,128)(2,1)} async-done(((bf16[128,1024]{1,0:T(8,128)(2,1)}), bf16[512,1024]{1,0:T(8,128)(2,1)}) %all-gather.2.cloned.1.call-update) | async-done | bytes 1048592 | tf_op jit(solution)/shard_map/all_gather | solution.py:79
  39.6 2.1 fusion.20
  41.7 1.2 reshape.234
  42.8 5.5 %fusion = (f32[2,64,4,16]{1,3,2,0:T(8,128)S(1)}, f32[2,4,4,64,64,16]{4,3,5,2,1,0:T(8,128)S(1)}) fusion(pred[2,64,4,64]{1,3,2,0:T(8,128)(4,1)S(1)} %broadcast_and_fusion, bf16[2,64,4,16,128,1]{4,3,2,1,0,5:T(8,128)(2,1)S(1)} %bitcast.51, bf16[4,2,64,4,128,1]{4,3,2,1,0,5:T(4,128)(2,1)S(1)} %bitcast.53), kind=kOutput, calls=%fused_computation.3 | convolution fusion | flops 543154176 | bytes 11075584 | tf_op jit(solution)/shard_map/sqgrd,nskgd->sqgrnk/dot_general | solution.py:102
  48.4 6.2 %fusion.3 = (f32[2,64,4,16]{1,3,2,0:T(8,128)S(1)}, bf16[2,64,4,16,4,64]{1,5,3,4,2,0:T(8,128)(2,1)}) fusion(f32[2,4,4,64,64,16]{4,3,5,2,1,0:T(8,128)S(1)} %get-tuple-element.14, f32[2,64,4,16]{1,3,2,0:T(8,128)S(1)} %broadcast_maximum_fusion, pred[2,64,4,64]{1,3,2,0:T(8,128)(4,1)S(1)} %broadcast_and_fusion), kind=kLoop, calls=%fused_computation.6 | loop fusion | flops 10477568 | bytes 12681216 | tf_op jit(solution)/shard_map/reduce_sum | solution.py:111
  54.6 0.1 reshape.236
  54.7 6.8 %fusion.8 = bf16[2,64,4,16,128]{4,1,3,2,0:T(8,128)(2,1)S(1)} fusion(bf16[2,64,4,16,4,64]{1,5,3,4,2,0:T(8,128)(2,1)} %get-tuple-element.6, f32[2,64,4,16]{1,3,2,0:T(8,128)S(1)} %get-tuple-element.10, f32[2,64,4,16]{1,3,2,0:T(8,128)S(1)} %get-tuple-element.9, bf16[4,2,64,4,128,1]{4,3,2,1,0,5:T(4,128)(2,1)S(1)} %bitcast.55), kind=kOutput, calls=%fused_computation.13 | convolution fusion | flops 540016640 | bytes 6881280 | tf_op jit(solution)/shard_map/sqgrnk,nskgd->sqgrd/dot_general | solution.py:113
  61.5 2.7 copy.14
  64.2 2.8 %reshape.237 = bf16[128,8192]{1,0:T(8,128)(2,1)S(1)} reshape(bf16[2,64,4,16,128]{4,3,2,1,0:T(8,128)(2,1)} %copy.14) | data formatting | bytes 4194304 | tf_op jit(solution)/shard_map/reshape | solution.py:117
  67.0 1.2 convolution_convert_fusion
  68.3 97.0 %all_to_all.5 = bf16[8,32,8192]{2,1,0:T(8,128)(2,1)S(1)} all-to-all(bf16[8,32,8192]{2,1,0:T(8,128)(2,1)S(1)} %bitcast.48), channel_id=1, replica_groups=mesh['pp'=4,'cp'=4,'tp'=2] {'cp','tp'}, dimensions={0} | all-to-all | bytes 8388608 | tf_op jit(solution)/shard_map/all_to_all | solution.py:40
  165.3 6.4 %copy.15 = bf16[4,2,32,8192]{3,1,2,0:T(2,128)(2,1)} copy(bf16[4,2,32,8192]{3,2,1,0:T(8,128)(2,1)S(1)} %bitcast.49) | data formatting | bytes 8388608 | tf_op jit(solution)/shard_map/reshape | solution.py:41
  171.6 4.8 %copy.29 = bf16[16,8,2,8192]{3,1,2,0:T(8,128)(2,1)S(1)} copy(bf16[16,8,2,8192]{3,2,1,0:T(2,128)(2,1)} %bitcast.50) | data formatting | bytes 8388608
  176.5 1.5 collective-permute-start
  178.0 91.4 %collective-permute-done = bf16[128,16384]{1,0:T(8,128)(2,1)S(1)} collective-permute-done((bf16[128,16384]{1,0:T(8,128)(2,1)S(1)}, bf16[128,16384]{1,0:T(8,128)(2,1)S(1)}, u32[]{:S(2)}, u32[]{:S(2)}) %collective-permute-start) | collective-permute-done | bytes 4194336 | tf_op jit(solution)/shard_map/ppermute | solution.py:13
  269.3 2.0 copy.47
  (12 shorter events, 0.1 us)
Async XLA Ops:
  6.5 8.7 %copy-start = (s32[4,128,1]{1,2,0:T(1,128)S(1)}, s32[4,128,1]{1,2,0:T(1,128)}, u32[]{:S(2)}) copy-start(s32[4,128,1]{1,2,0:T(1,128)} %param.11) | copy-start | bytes 6148
  6.5 33.1 %all-gather.2.cloned.1.call-start = ((), (), s32[]{:S(2)}) async-start(), calls=%async_computation.1 | async-start | bytes 1310720 | tf_op jit(solution)/shard_map/all_gather | solution.py:79
  176.5 92.9 %collective-permute-start = (bf16[128,16384]{1,0:T(8,128)(2,1)S(1)}, bf16[128,16384]{1,0:T(8,128)(2,1)S(1)}, u32[]{:S(2)}, u32[]{:S(2)}) collective-permute-start(bf16[128,16384]{1,0:T(8,128)(2,1)S(1)} %bitcast.52), channel_id=1, source_target_pairs={{24,0},{0,8},{8,16},{16,24},{25,1},{1,9},{9,17},{17,25},{26,2},{2,... | collective-permute-start | bytes 12582920 | tf_op jit(solution)/shard_map/ppermute | solution.py:13
Sparse Core Ops, SparseCore 0:
  8.9 30.6 all-gather.1
